TPU v7x, 32 devices: a whole 2x2x4 slice. The times are simulated.
32 devices in a mesh: row: 8 (over z, y), col: 4 (over x, core).
Axes of the slice: x: 2, y: 2, z: 4, core: 2. Of those that a mesh axis runs over, the one named last changes fastest.
Arguments:
- trailing: bfloat16 [12288, 12288], P('row', 'col'), may hold values from -6 to 6
- rows_a: int32 [8, 12], replicated, may hold values from 0 to 11, as said below
- counts_a: int32 [8], replicated, may hold values from 1 to 12, as said below
- factor_a: bfloat16 [12288, 512], P('row'), may hold values from -0.0546875 to 0.0546875
- rows_b: int32 [8, 12], replicated, may hold values from 0 to 11, as said below
- counts_b: int32 [8], replicated, may hold values from 1 to 12, as said below
- factor_b: bfloat16 [12288, 512], P('row'), may hold values from -0.0546875 to 0.0546875
- factor_top: bfloat16 [512, 512], replicated, may hold values from -0.25 to 0.25
- base_a: float32 [512, 512], P('col'), may hold values from -3 to 3
- base_b: float32 [512, 512], P('col'), may hold values from -3 to 3
Outputs:
- column_a: bfloat16 [12288, 512], P('row')
- diag_a: float32 [512, 512], P('col')
- column_b: bfloat16 [12288, 512], P('row')
- top_b: bfloat16 [512, 512], P('col')
- diag_b: float32 [512, 512], P('col')
Inputs may be any that keep to these rules, and one draw needn't show every extreme that they name: `rows_a`: the first counts_a[r] entries of row r are distinct; the rest of the row is padding. `counts_a`: some owner uses all 12 slots in every draw. `rows_b`: the first counts_b[r] entries of row r are distinct and lie among the first counts_a[r] entries of row r of rows_a; the rest is padding. counts_b[r] <= counts_a[r]; some owner uses all 12 slots in every draw.
All inputs are finite; a program needn't handle non-finite values.
Results may differ from a plain program's by a relative error of at most 0.007.
Values may be sent and summed in bfloat16 or wider, within the bound.
A program may use at most 128 MiB of HBM per device.

v0:
```python
import jax
import jax.numpy as jnp
from jax import lax
from jax.sharding import PartitionSpec as P


def contract_rows(former, latter):
    return lax.dot_general(
        former, latter, (((0,), (0,)), ((), ())), preferred_element_type=jnp.float32
    )


def on_device(
    trailing, rows_a, counts_a, factor_a, rows_b, counts_b, factor_b, factor_top, base_a, base_b
):
    row_count = lax.axis_size("row")
    col_count = lax.axis_size("col")
    fanout = row_count // col_count
    row_index = lax.axis_index("row")
    col_index = lax.axis_index("col")
    slots = rows_a.shape[1]
    total_rows, width = factor_a.shape
    block = total_rows // slots
    row_blocks = trailing.shape[0] // block
    part_width = width // col_count
    width_start = col_index * part_width
    slot_ids = jnp.arange(slots, dtype=jnp.int32)

    def own(table):
        return lax.dynamic_index_in_dim(table, row_index, 0, keepdims=False)

    live_a = slot_ids < own(counts_a)
    live_b = slot_ids < own(counts_b)
    own_a, own_b = (own(rows_a), own(rows_b))
    blocks = jnp.arange(row_blocks, dtype=jnp.int32)
    gate_a = jnp.any((own_a[None, :] == blocks[:, None]) & live_a[None, :], axis=1)
    gate_b = jnp.any((own_b[None, :] == blocks[:, None]) & live_b[None, :], axis=1)
    pieces = jnp.stack([factor_a, factor_b]).reshape(2, row_count, total_rows // row_count, width)
    arrived = []
    for shift in range(row_count):
        piece = lax.dynamic_index_in_dim(pieces, (row_index + shift) % row_count, 1, keepdims=False)
        if shift:
            pairs = [
                (
                    owner * col_count + owner % col_count,
                    (owner + shift) % row_count * col_count + owner % col_count,
                )
                for owner in range(row_count)
            ]
            piece = lax.ppermute(piece, ("row", "col"), pairs)
        arrived.append(piece)
    arrived = jnp.stack(arrived)
    mine = jnp.stack(
        [
            lax.dynamic_index_in_dim(
                arrived, (row_index - col_index - part * col_count) % row_count, 0, keepdims=False
            )
            for part in range(fanout)
        ],
        axis=1,
    )
    held = lax.all_gather(mine, "row", axis=2, tiled=True)
    owners = col_index + jnp.arange(fanout, dtype=jnp.int32) * col_count

    def partial_product(node, rows, counts):
        own_rows = jnp.take(rows, owners, axis=0)
        live = slot_ids[None, :] < jnp.take(counts, owners, axis=0)[:, None]
        match = (own_rows[None, :, :] == blocks[:, None, None]) & live[None, :, :]
        filled = jnp.any(match, axis=2).reshape(-1)
        source = jnp.argmax(match, axis=2).astype(jnp.int32)
        source = (source + jnp.arange(fanout, dtype=jnp.int32) * slots).reshape(-1)
        picked = jnp.take(held[node].reshape(fanout * slots, block, width), source, axis=0)
        spread = jnp.where(filled[:, None, None], picked, 0).reshape(-1, width)
        return jnp.dot(trailing, spread, preferred_element_type=jnp.float32).astype(jnp.bfloat16)

    part = jnp.stack([partial_product(0, rows_a, counts_a), partial_product(1, rows_b, counts_b)])
    reduced = lax.psum_scatter(part, "col", scatter_dimension=2, tiled=True).astype(jnp.float32)

    def gated(value, gate):
        return jnp.where(gate[:, None, None], value.reshape(row_blocks, block, -1), 0).reshape(
            row_blocks * block, -1
        )

    def by_slot(value, own_rows, live):
        picked = jnp.take(value.reshape(row_blocks, block, -1), own_rows, axis=0)
        return jnp.where(live[:, None, None], picked, 0).reshape(total_rows, -1)

    col_a = gated(-reduced[0], gate_a).astype(jnp.bfloat16)
    whole_a = lax.all_gather(col_a, "col", axis=1, tiled=True)
    column_a = by_slot(whole_a, own_a, live_a)
    top_part = lax.dynamic_slice_in_dim(factor_top, width_start, part_width, 1)
    cross = jnp.dot(whole_a, top_part, preferred_element_type=jnp.float32)
    col_b = gated(-(reduced[1] + cross), gate_b).astype(jnp.bfloat16)
    column_b = by_slot(lax.all_gather(col_b, "col", axis=1, tiled=True), own_b, live_b)
    sums = lax.psum(
        (
            contract_rows(by_slot(col_a, own_a, live_a), factor_a),
            contract_rows(by_slot(col_a, own_b, live_b), factor_b),
            contract_rows(by_slot(col_b, own_b, live_b), factor_b),
        ),
        "row",
    )
    diag_a = base_a - sums[0]
    top_b = (
        -(
            sums[1]
            + jnp.dot(diag_a, factor_top.astype(jnp.float32), precision=lax.Precision.HIGHEST)
        )
    ).astype(jnp.bfloat16)
    top_whole = lax.all_gather(top_b, "col", axis=0, tiled=True)
    top_cols = lax.dynamic_slice_in_dim(top_whole, width_start, part_width, 1)
    diag_b = base_b - sums[2] - contract_rows(top_cols, factor_top)
    return (column_a, diag_a, column_b, top_b, diag_b)


def solution(mesh):
    in_specs = (
        P("row", "col"),
        P(),
        P(),
        P("row", None),
        P(),
        P(),
        P("row", None),
        P(),
        P("col", None),
        P("col", None),
    )
    out_specs = (P("row", None), P("col", None), P("row", None), P("col", None), P("col", None))
    return jax.shard_map(
        on_device, mesh=mesh, in_specs=in_specs, out_specs=out_specs, check_vma=False
    )
```

profile of v0, /device:TPU:0, one launch (start us, length us, event | category | flops | bytes accessed | tf_op | source)
XLA Modules:
  0.0 359.1 jit_solution(10162166294966140)
XLA Ops:
  7.3 2.9 fusion.22
  10.2 5.7 %collective-permute-start = (bf16[2,192,512]{2,1,0:T(8,128)(2,1)}, bf16[2,192,512]{2,1,0:T(8,128)(2,1)}, u32[]{:S(2)}, u32[]{:S(2)}) collective-permute-start(bf16[2,192,512]{2,1,0:T(8,128)(2,1)} %get-tuple-element.26), channel_id=1, source_target_pairs={{0,4},{5,9},{10,14},{15,19},{16,20},{21,25},{26,30},{31,3}} | collective-permute-start | bytes 1179656 | tf_op jit(solution)/shard_map/ppermute | solution.py:50
  15.9 2.1 collective-permute-start.1
  18.0 2.0 collective-permute-start.2
  20.0 4.5 %collective-permute-start.3 = (bf16[2,192,512]{2,1,0:T(8,128)(2,1)S(1)}, bf16[2,192,512]{2,1,0:T(8,128)(2,1)}, u32[]{:S(2)}, u32[]{:S(2)}) collective-permute-start(bf16[2,192,512]{2,1,0:T(8,128)(2,1)S(1)} %get-tuple-element.29), channel_id=1, source_target_pairs={{0,16},{5,21},{10,26},{15,31},{16,0},{21,5},{26,10},{31,15}} | collective-permute-start | bytes 1179656 | tf_op jit(solution)/shard_map/ppermute | solution.py:50
  24.5 2.1 collective-permute-start.4
  26.6 1.7 bitcast_dynamic-update-slice_fusion.7
  28.2 1.1 fusion.16
  29.4 1.3 collective-permute-start.5
  30.7 1.0 bitcast_dynamic-update-slice_fusion.6
  31.7 1.3 collective-permute-start.6
  33.1 1.0 bitcast_dynamic-update-slice_fusion.5
  36.2 1.0 bitcast_dynamic-update-slice_fusion.2
  37.3 2.3 collective-permute-done.5
  39.6 4.2 %collective-permute-done.6 = bf16[2,192,512]{2,1,0:T(8,128)(2,1)S(1)} collective-permute-done((bf16[2,192,512]{2,1,0:T(8,128)(2,1)S(1)}, bf16[2,192,512]{2,1,0:T(8,128)(2,1)S(1)}, u32[]{:S(2)}, u32[]{:S(2)}) %collective-permute-start.6) | collective-permute-done | bytes 393248 | tf_op jit(solution)/shard_map/ppermute | solution.py:50
  47.6 1.1 iota_reduce_fusion.1
  48.7 1.1 iota_reduce_fusion
  50.7 95.2 %all-gather.4.cloned.1.call-done = bf16[2,2,1536,512]{3,2,0,1:T(8,128)(2,1)} async-done(((bf16[2,2,192,512]{3,2,0,1:T(8,128)(2,1)}), bf16[2,2,1536,512]{3,2,0,1:T(8,128)(2,1)}) %all-gather.4.cloned.1.call-update) | async-done | bytes 6291472 | tf_op jit(solution)/shard_map/all_gather | solution.py:62
  145.9 5.9 %fusion.37 = (bf16[1,2,1536,512]{3,2,0,1:T(8,128)(2,1)}, bf16[1,2,1536,512]{3,2,0,1:T(8,128)(2,1)}) fusion(bf16[2,2,1536,512]{3,2,0,1:T(8,128)(2,1)} %all-gather.4.cloned.1.call-done), kind=kLoop, calls=%fused_computation.126 | loop fusion | bytes 12582912 | tf_op jit(solution)/shard_map/slice | solution.py:72
  151.8 4.4 %gather_fusion.2 = bf16[24,128,512]{2,1,0:T(8,128)(2,1)} fusion(bf16[24,128,512]{2,1,0:T(8,128)(2,1)} %bitcast.98, s32[1024]{0:T(1024)S(1)} %pad_clamp_fusion.3), kind=kCustom, calls=%fused_computation.2.clone | custom fusion | bytes 6291552 | tf_op jit(solution)/shard_map/jit(_take)/gather | solution.py:72
  156.2 2.3 select_select_fusion.1
  158.5 9.0 %fusion = bf16[1,1536,512]{1,2,0:T(8,128)(2,1)} fusion(bf16[3072,512]{1,0:T(8,128)(2,1)S(1)} %bitcast.101, bf16[1536,3072]{1,0:T(8,128)(2,1)} %param.20), kind=kOutput, calls=%fused_computation.32 | convolution fusion | flops 4832624640 | bytes 14155776 | tf_op jit(solution)/shard_map/dot_general | solution.py:74
  167.5 4.4 %gather_fusion.5 = bf16[24,128,512]{2,1,0:T(8,128)(2,1)} fusion(bf16[24,128,512]{2,1,0:T(8,128)(2,1)} %bitcast.97, s32[1024]{0:T(1024)S(1)} %pad_clamp_fusion.2), kind=kCustom, calls=%fused_computation.7.clone | custom fusion | bytes 6291552 | tf_op jit(solution)/shard_map/jit(_take)/gather | solution.py:72
  171.9 2.3 select_select_fusion
  174.2 8.0 %fusion.1 = bf16[1,1536,512]{1,2,0:T(8,128)(2,1)S(1)} fusion(bf16[3072,512]{1,0:T(8,128)(2,1)S(1)} %bitcast.102, bf16[1536,3072]{1,0:T(8,128)(2,1)} %param.20), kind=kOutput, calls=%fused_computation.33 | convolution fusion | flops 4832624640 | bytes 14155776 | tf_op jit(solution)/shard_map/dot_general | solution.py:74
  182.2 1.9 pad_maximum_fusion
  186.2 34.1 %reduce-scatter.2.cloned.1.call-done = bf16[2,1536,128]{1,2,0:T(8,128)(2,1)} async-done(((bf16[2,1536,512]{1,2,0:T(8,128)(2,1)}), bf16[2,1536,128]{1,2,0:T(8,128)(2,1)}) %reduce-scatter.2.cloned.1.call-update) | async-done | bytes 786448 | tf_op jit(solution)/shard_map/reduce_scatter | solution.py:77
  220.3 1.3 convert_element_type.45
  221.6 1.1 copy-done.4
  224.7 1.2 slice_negate_fusion
  227.7 2.5 fusion.38
  230.2 13.2 %all-gather.6.cloned.1.call-done = bf16[1536,512]{0,1:T(8,128)(2,1)} async-done(((bf16[1536,128]{0,1:T(8,128)(2,1)}), bf16[1536,512]{0,1:T(8,128)(2,1)}) %all-gather.6.cloned.1.call-update) | async-done | bytes 1572880 | tf_op jit(solution)/shard_map/all_gather | solution.py:89
  243.4 2.0 fusion.4
  245.7 1.4 gather_fusion.10
  247.1 1.2 select_select_fusion.4
  248.2 1.1 fusion.39
  249.3 1.1 fusion.40
  251.1 2.6 copy.27
  253.7 2.1 gather_fusion.6
  255.8 1.4 select_select_fusion.3
  257.2 69.1 %all-reduce.3.cloned.1.call-done = (f32[128,512]{1,0:T(8,128)}, f32[128,512]{1,0:T(8,128)}, f32[128,512]{1,0:T(8,128)}) async-done(((f32[128,512]{1,0:T(8,128)}, f32[128,512]{1,0:T(8,128)}, f32[128,512]{1,0:T(8,128)}), (f32[128,512]{1,0:T(8,128)}, f32[128,512]{1,0:T(8,128)}, f32[128,512]{1,0:T(8,128)})) %all-reduce.3.cloned.1.call-update) | async-done | bytes 786448 | tf_op jit(solution)/shard_map/psum | solution.py:95
  327.3 1.4 fusion.6
  328.7 7.1 %all_gather.15 = bf16[512,512]{1,0:T(8,128)(2,1)S(1)} all-gather(bf16[128,512]{1,0:T(8,128)(2,1)S(1)} %fusion.6), channel_id=1, replica_groups=mesh['row'=8,'col'=4] {'col'}, dimensions={0}, use_global_device_ids=true | all-gather | bytes 655360 | tf_op jit(solution)/shard_map/all_gather | solution.py:110
  335.9 1.9 convolution_subtract_fusion
  337.8 8.7 %all-gather.8.cloned.1.call-done = bf16[1536,512]{0,1:T(8,128)(2,1)} async-done(((bf16[1536,128]{0,1:T(8,128)(2,1)}), bf16[1536,512]{0,1:T(8,128)(2,1)}) %all-gather.8.cloned.1.call-update) | async-done | bytes 1572880 | tf_op jit(solution)/shard_map/all_gather | solution.py:94
  346.5 2.6 copy.30
  349.1 2.1 gather_fusion.8
  351.2 1.4 select_select_fusion.2
  (92 shorter events, 14.4 us)
Async XLA Ops:
  7.2 236.2 %copy-start = (bf16[512,512]{1,0:T(8,128)(2,1)S(1)}, bf16[512,512]{1,0:T(8,128)(2,1)}, u32[]{:S(2)}) copy-start(bf16[512,512]{1,0:T(8,128)(2,1)} %param.27) | copy-start | bytes 1572868
  7.2 19.4 %copy-start.3 = (bf16[1536,512]{1,0:T(8,128)(2,1)S(1)}, bf16[1536,512]{1,0:T(8,128)(2,1)}, u32[]{:S(2)}) copy-start(bf16[1536,512]{1,0:T(8,128)(2,1)} %param.26) | copy-start | bytes 4718596
  7.2 138.7 %all-gather.4.cloned.1.call-start = ((), (), s32[]{:S(2)}) async-start(), calls=%async_computation.1 | async-start | bytes 7077888 | tf_op jit(solution)/shard_map/all_gather | solution.py:62
  10.2 19.1 %collective-permute-start = (bf16[2,192,512]{2,1,0:T(8,128)(2,1)}, bf16[2,192,512]{2,1,0:T(8,128)(2,1)}, u32[]{:S(2)}, u32[]{:S(2)}) collective-permute-start(bf16[2,192,512]{2,1,0:T(8,128)(2,1)} %get-tuple-element.26), channel_id=1, source_target_pairs={{0,4},{5,9},{10,14},{15,19},{16,20},{21,25},{26,30},{31,3}} | collective-permute-start | bytes 1179656 | tf_op jit(solution)/shard_map/ppermute | solution.py:50
  15.9 15.8 %collective-permute-start.1 = (bf16[2,192,512]{2,1,0:T(8,128)(2,1)}, bf16[2,192,512]{2,1,0:T(8,128)(2,1)}, u32[]{:S(2)}, u32[]{:S(2)}) collective-permute-start(bf16[2,192,512]{2,1,0:T(8,128)(2,1)} %get-tuple-element.27), channel_id=1, source_target_pairs={{0,8},{5,13},{10,18},{15,23},{16,24},{21,29},{26,2},{31,7}} | collective-permute-start | bytes 1179656 | tf_op jit(solution)/shard_map/ppermute | solution.py:50
  18.0 16.1 %collective-permute-start.2 = (bf16[2,192,512]{2,1,0:T(8,128)(2,1)}, bf16[2,192,512]{2,1,0:T(8,128)(2,1)}, u32[]{:S(2)}, u32[]{:S(2)}) collective-permute-start(bf16[2,192,512]{2,1,0:T(8,128)(2,1)} %get-tuple-element.28), channel_id=1, source_target_pairs={{0,12},{5,17},{10,22},{15,27},{16,28},{21,1},{26,6},{31,11}} | collective-permute-start | bytes 1179656 | tf_op jit(solution)/shard_map/ppermute | solution.py:50
  20.0 15.1 %collective-permute-start.3 = (bf16[2,192,512]{2,1,0:T(8,128)(2,1)S(1)}, bf16[2,192,512]{2,1,0:T(8,128)(2,1)}, u32[]{:S(2)}, u32[]{:S(2)}) collective-permute-start(bf16[2,192,512]{2,1,0:T(8,128)(2,1)S(1)} %get-tuple-element.29), channel_id=1, source_target_pairs={{0,16},{5,21},{10,26},{15,31},{16,0},{21,5},{26,10},{31,15}} | collective-permute-start | bytes 1179656 | tf_op jit(solution)/shard_map/ppermute | solution.py:50
  24.5 11.7 %collective-permute-start.4 = (bf16[2,192,512]{2,1,0:T(8,128)(2,1)S(1)}, bf16[2,192,512]{2,1,0:T(8,128)(2,1)}, u32[]{:S(2)}, u32[]{:S(2)}) collective-permute-start(bf16[2,192,512]{2,1,0:T(8,128)(2,1)S(1)} %get-tuple-element.30), channel_id=1, source_target_pairs={{0,20},{5,25},{10,30},{15,3},{16,4},{21,9},{26,14},{31,19}} | collective-permute-start | bytes 1179656 | tf_op jit(solution)/shard_map/ppermute | solution.py:50
  28.2 2.5 copy-start.9
  29.4 10.2 %collective-permute-start.5 = (bf16[2,192,512]{2,1,0:T(8,128)(2,1)S(1)}, bf16[2,192,512]{2,1,0:T(8,128)(2,1)S(1)}, u32[]{:S(2)}, u32[]{:S(2)}) collective-permute-start(bf16[2,192,512]{2,1,0:T(8,128)(2,1)S(1)} %fusion.16), channel_id=1, source_target_pairs={{0,24},{5,29},{10,2},{15,7},{16,8},{21,13},{26,18},{31,23}} | collective-permute-start | bytes 1179656 | tf_op jit(solution)/shard_map/ppermute | solution.py:50
  31.7 12.0 %collective-permute-start.6 = (bf16[2,192,512]{2,1,0:T(8,128)(2,1)S(1)}, bf16[2,192,512]{2,1,0:T(8,128)(2,1)S(1)}, u32[]{:S(2)}, u32[]{:S(2)}) collective-permute-start(bf16[2,192,512]{2,1,0:T(8,128)(2,1)S(1)} %get-tuple-element.25), channel_id=1, source_target_pairs={{0,28},{5,1},{10,6},{15,11},{16,12},{21,17},{26,22},{31,27}} | collective-permute-start | bytes 1179656 | tf_op jit(solution)/shard_map/ppermute | solution.py:50
  36.2 8.7 %copy-start.12 = (s32[8,12]{1,0:T(8,128)S(1)}, s32[8,12]{1,0:T(8,128)}, u32[]{:S(2)}) copy-start(s32[8,12]{1,0:T(8,128)} %param.21) | copy-start | bytes 1156
  36.2 9.3 %copy-start.13 = (s32[8,12]{1,0:T(8,128)S(1)}, s32[8,12]{1,0:T(8,128)}, u32[]{:S(2)}) copy-start(s32[8,12]{1,0:T(8,128)} %param.24) | copy-start | bytes 1156
  36.2 9.8 %copy-start.1 = (s32[8]{0:T(128)S(1)}, s32[8]{0:T(128)}, u32[]{:S(2)}) copy-start(s32[8]{0:T(128)} %param.22) | copy-start | bytes 100
  37.2 9.4 %copy-start.2 = (s32[8]{0:T(128)S(1)}, s32[8]{0:T(128)}, u32[]{:S(2)}) copy-start(s32[8]{0:T(128)} %param.25) | copy-start | bytes 100
  44.8 175.5 %reduce-scatter.2.cloned.1.call-start = ((), (), s32[]{:S(2)}) async-start(), calls=%async_computation.2 | async-start | bytes 3932160 | tf_op jit(solution)/shard_map/reduce_scatter | solution.py:77
  174.2 8.0 %copy-start.6 = (bf16[1,1536,512]{1,2,0:T(8,128)(2,1)S(1)}, bf16[1,1536,512]{1,2,0:T(8,128)(2,1)}, u32[]{:S(2)}) copy-start(bf16[1,1536,512]{1,2,0:T(8,128)(2,1)} %fusion) | copy-start | bytes 4718596
  184.1 59.3 %all-gather.6.cloned.1.call-start = ((), (), s32[]{:S(2)}) async-start(), calls=%async_computation.3 | async-start | bytes 1966080 | tf_op jit(solution)/shard_map/all_gather | solution.py:89
  221.6 1.1 copy-start.4
  223.6 102.7 %all-reduce.3.cloned.1.call-start = ((), (), s32[]{:S(2)}) async-start(), calls=%async_computation.5 | async-start | bytes 1572864 | tf_op jit(solution)/shard_map/psum | solution.py:95
  245.5 5.0 %copy-start.5 = (bf16[1536,128]{0,1:T(8,128)(2,1)}, bf16[1536,128]{0,1:T(8,128)(2,1)S(1)}, u32[]{:S(2)}) copy-start(bf16[1536,128]{0,1:T(8,128)(2,1)S(1)} %fusion.4) | copy-start | bytes 1179652
  250.5 96.0 %all-gather.8.cloned.1.call-start = ((), (), s32[]{:S(2)}) async-start(), calls=%async_computation.4 | async-start | bytes 1966080 | tf_op jit(solution)/shard_map/all_gather | solution.py:94
  253.7 72.6 %copy-start.10 = (f32[128,512]{1,0:T(8,128)S(1)}, f32[128,512]{1,0:T(8,128)}, u32[]{:S(2)}) copy-start(f32[128,512]{1,0:T(8,128)} %param.28) | copy-start | bytes 786436
  255.8 80.1 %copy-start.11 = (f32[128,512]{1,0:T(8,128)S(1)}, f32[128,512]{1,0:T(8,128)}, u32[]{:S(2)}) copy-start(f32[128,512]{1,0:T(8,128)} %param.29) | copy-start | bytes 786436
  327.3 21.8 %copy-start.7 = (f32[128,512]{1,0:T(8,128)}, f32[128,512]{1,0:T(8,128)S(1)}, u32[]{:S(2)}) copy-start(f32[128,512]{1,0:T(8,128)S(1)} %sub.18) | copy-start | bytes 786436
  328.7 22.4 %copy-start.8 = (bf16[128,512]{1,0:T(8,128)(2,1)}, bf16[128,512]{1,0:T(8,128)(2,1)S(1)}, u32[]{:S(2)}) copy-start(bf16[128,512]{1,0:T(8,128)(2,1)S(1)} %fusion.6) | copy-start | bytes 393220
Sparse Core Ops, SparseCore 0:
  44.9 100.8 all-gather.3
  184.2 36.0 reduce-scatter.1
  223.7 19.6 all-gather.5
  250.6 75.6 all-reduce.2
  327.7 18.7 all-gather.7
where the time goes:
time: 360 us; the launch traced here: 359 us
  waiting for transfers between devices  227 us (63%)
  local copies, waits for them, and re-layouts  37.5 us (10%)
  matrix products  27.1 us (8%)
  other arithmetic  26.2 us (7%)
  starting transfers between devices  19.3 us (5%)
  between operations  14.4 us (4%)
  blocking collectives  7.15 us (2%)
    all_gather x1, waiting for transfers between devices, on_device(): held = lax.all_gather(mine, 'row', axis=2, tiled=True)  95.2 us
    psum x1, waiting for transfers between devices, on_device(): lax.psum((contract_rows(by_slot(col_a, own_a, live_a), factor_a), contrac...  69.1 us
    reduce_scatter x1, waiting for transfers between devices, on_device(): lax.psum_scatter(part, 'col', scatter_dimension=2, tiled=True)  34.1 us
    ppermute x7, starting transfers between devices, on_device(): piece = lax.ppermute(piece, ('row', 'col'), pairs)  18.9 us
    dot_general x2, matrix products, partial_product(): jnp.dot(trailing, spread, preferred_element_type=jnp.float32)  17 us
    all_gather x1, waiting for transfers between devices, on_device(): whole_a = lax.all_gather(col_a, 'col', axis=1, tiled=True)  13.2 us
    gather x2, local copies, waits for them, and re-layouts, partial_product(): jnp.take(held[node].reshape(fanout * slots, block, width), source, axis=0)  8.76 us
    all_gather x1, waiting for transfers between devices, on_device(): lax.all_gather(col_b, 'col', axis=1, tiled=True)  8.72 us
  transfers between devices with their start and end apart: 12, of which 7 were waited for; matrix products, arithmetic and copies ran while one was open for 9% of the time, Pallas kernels for 0%

commit v1 on v0

--- a/solution.py
+++ b/solution.py
@@ -59,7 +59,12 @@
         ],
         axis=1,
     )
-    held = lax.all_gather(mine, "row", axis=2, tiled=True)
+    ring = [mine]
+    for hop in range(7):
+        ring.append(lax.ppermute(ring[-1], "row", [(dev, (dev + 1) % 8) for dev in range(8)]))
+    held = jnp.roll(
+        jnp.concatenate(ring[::-1], axis=2), (lax.axis_index("row") + 1) * ring[0].shape[2], axis=2
+    )
     owners = col_index + jnp.arange(fanout, dtype=jnp.int32) * col_count
 
     def partial_product(node, rows, counts):

time: 360 us -> 410 us (1.14)
  waiting for transfers between devices: 227 us -> 260 us
  local copies, waits for them, and re-layouts: 37.5 us -> 49.8 us
  starting transfers between devices: 19.3 us -> 24.5 us
    ppermute x0 -> x7, waiting for transfers between devices: none -> 116 us  [on_device(): lax.ppermute(ring[-1], 'row', [(dev, (dev + 1) % 8) for dev in range(8)])]
    all_gather x1 -> x0, waiting for transfers between devices: 95.2 us -> none  [on_device(): held = lax.all_gather(mine, 'row', axis=2, tiled=True)]
    unnamed x34 -> x56, local copies, waits for them, and re-layouts: 6.36 us -> 20.3 us
    reduce_scatter x1, waiting for transfers between devices: 34.1 us -> 46.6 us  [on_device(): lax.psum_scatter(part, 'col', scatter_dimension=2, tiled=True)]
    ppermute x0 -> x7, starting transfers between devices: none -> 5.17 us  [on_device(): lax.ppermute(ring[-1], 'row', [(dev, (dev + 1) % 8) for dev in range(8)])]
  transfers between devices with their start and end apart: 12 -> 18, of which waited for: 7 -> 13; matrix products, arithmetic and copies ran while one was open for 9% -> 8% of each run, Pallas kernels for 0% -> 0%
where the time goes in v1:
time: 410 us; the launch traced here: 409 us
  waiting for transfers between devices  260 us (63%)
  local copies, waits for them, and re-layouts  49.8 us (12%)
  matrix products  27.1 us (7%)
  other arithmetic  25.5 us (6%)
  starting transfers between devices  24.5 us (6%)
  between operations  14.5 us (4%)
  blocking collectives  7.15 us (2%)
    ppermute x7, waiting for transfers between devices, on_device(): lax.ppermute(ring[-1], 'row', [(dev, (dev + 1) % 8) for dev in range(8)])  116 us
    psum x1, waiting for transfers between devices, on_device(): lax.psum((contract_rows(by_slot(col_a, own_a, live_a), factor_a), contrac...  69.1 us
    reduce_scatter x1, waiting for transfers between devices, on_device(): lax.psum_scatter(part, 'col', scatter_dimension=2, tiled=True)  46.6 us
    unnamed x56, local copies, waits for them, and re-layouts  20.3 us
    ppermute x7, starting transfers between devices, on_device(): piece = lax.ppermute(piece, ('row', 'col'), pairs)  18.9 us
    dot_general x2, matrix products, partial_product(): jnp.dot(trailing, spread, preferred_element_type=jnp.float32)  17 us
    all_gather x1, waiting for transfers between devices, on_device(): whole_a = lax.all_gather(col_a, 'col', axis=1, tiled=True)  13.1 us
    gather x2, local copies, waits for them, and re-layouts, partial_product(): jnp.take(held[node].reshape(fanout * slots, block, width), source, axis=0)  8.87 us
  transfers between devices with their start and end apart: 18, of which 13 were waited for; matrix products, arithmetic and copies ran while one was open for 8% of the time, Pallas kernels for 0%

profile of v1, /device:TPU:0, one launch (start us, length us, event | category | flops | bytes accessed | tf_op | source)
XLA Modules:
  0.0 408.9 jit_solution(918490085836492734)
XLA Ops:
  7.3 2.9 fusion.22
  10.2 5.6 %collective-permute-start = (bf16[2,192,512]{2,1,0:T(8,128)(2,1)}, bf16[2,192,512]{2,1,0:T(8,128)(2,1)}, u32[]{:S(2)}, u32[]{:S(2)}) collective-permute-start(bf16[2,192,512]{2,1,0:T(8,128)(2,1)} %get-tuple-element.26), channel_id=1, source_target_pairs={{0,4},{5,9},{10,14},{15,19},{16,20},{21,25},{26,30},{31,3}} | collective-permute-start | bytes 1179656 | tf_op jit(solution)/shard_map/ppermute | solution.py:50
  15.9 2.0 collective-permute-start.1
  17.9 2.0 collective-permute-start.2
  20.0 4.5 %collective-permute-start.3 = (bf16[2,192,512]{2,1,0:T(8,128)(2,1)S(1)}, bf16[2,192,512]{2,1,0:T(8,128)(2,1)}, u32[]{:S(2)}, u32[]{:S(2)}) collective-permute-start(bf16[2,192,512]{2,1,0:T(8,128)(2,1)S(1)} %get-tuple-element.29), channel_id=1, source_target_pairs={{0,16},{5,21},{10,26},{15,31},{16,0},{21,5},{26,10},{31,15}} | collective-permute-start | bytes 1179656 | tf_op jit(solution)/shard_map/ppermute | solution.py:50
  24.5 2.1 collective-permute-start.4
  26.5 1.7 bitcast_dynamic-update-slice_fusion.7
  29.4 1.3 collective-permute-start.5
  31.7 1.3 collective-permute-start.6
  37.3 2.3 collective-permute-done.5
  39.5 4.2 %collective-permute-done.6 = bf16[2,192,512]{2,1,0:T(8,128)(2,1)S(1)} collective-permute-done((bf16[2,192,512]{2,1,0:T(8,128)(2,1)S(1)}, bf16[2,192,512]{2,1,0:T(8,128)(2,1)S(1)}, u32[]{:S(2)}, u32[]{:S(2)}) %collective-permute-start.6) | collective-permute-done | bytes 393248 | tf_op jit(solution)/shard_map/ppermute | solution.py:50
  44.0 19.9 %collective-permute-done.7 = bf16[2,2,192,512]{3,2,0,1:T(8,128)(2,1)S(1)} collective-permute-done((bf16[2,2,192,512]{3,2,0,1:T(8,128)(2,1)S(1)}, bf16[2,2,192,512]{3,2,0,1:T(8,128)(2,1)S(1)}, u32[]{:S(2)}, u32[]{:S(2)}) %collective-permute-start.7) | collective-permute-done | bytes 786464 | tf_op jit(solution)/shard_map/ppermute | solution.py:64
  64.8 18.6 %collective-permute-done.8 = bf16[2,2,192,512]{3,2,0,1:T(8,128)(2,1)S(1)} collective-permute-done((bf16[2,2,192,512]{3,2,0,1:T(8,128)(2,1)S(1)}, bf16[2,2,192,512]{3,2,0,1:T(8,128)(2,1)S(1)}, u32[]{:S(2)}, u32[]{:S(2)}) %collective-permute-start.8) | collective-permute-done | bytes 786464 | tf_op jit(solution)/shard_map/ppermute | solution.py:64
  84.3 17.9 %collective-permute-done.9 = bf16[2,2,192,512]{3,2,0,1:T(8,128)(2,1)} collective-permute-done((bf16[2,2,192,512]{3,2,0,1:T(8,128)(2,1)S(1)}, bf16[2,2,192,512]{3,2,0,1:T(8,128)(2,1)}, u32[]{:S(2)}, u32[]{:S(2)}) %collective-permute-start.9) | collective-permute-done | bytes 786464 | tf_op jit(solution)/shard_map/ppermute | solution.py:64
  102.8 16.8 %collective-permute-done.10 = bf16[2,2,192,512]{3,2,0,1:T(8,128)(2,1)} collective-permute-done((bf16[2,2,192,512]{3,2,0,1:T(8,128)(2,1)}, bf16[2,2,192,512]{3,2,0,1:T(8,128)(2,1)}, u32[]{:S(2)}, u32[]{:S(2)}) %collective-permute-start.10) | collective-permute-done | bytes 786464 | tf_op jit(solution)/shard_map/ppermute | solution.py:64
  122.4 13.8 %collective-permute-done.11 = bf16[2,2,192,512]{3,2,0,1:T(8,128)(2,1)} collective-permute-done((bf16[2,2,192,512]{3,2,0,1:T(8,128)(2,1)}, bf16[2,2,192,512]{3,2,0,1:T(8,128)(2,1)}, u32[]{:S(2)}, u32[]{:S(2)}) %collective-permute-start.11) | collective-permute-done | bytes 786464 | tf_op jit(solution)/shard_map/ppermute | solution.py:64
  136.2 2.6 collective-permute-start.12
  141.1 13.7 %collective-permute-done.12 = bf16[2,2,192,512]{3,2,0,1:T(8,128)(2,1)} collective-permute-done((bf16[2,2,192,512]{3,2,0,1:T(8,128)(2,1)}, bf16[2,2,192,512]{3,2,0,1:T(8,128)(2,1)}, u32[]{:S(2)}, u32[]{:S(2)}) %collective-permute-start.12) | collective-permute-done | bytes 786464 | tf_op jit(solution)/shard_map/ppermute | solution.py:64
  154.8 1.7 collective-permute-start.13
  157.2 15.3 %collective-permute-done.13 = bf16[2,2,192,512]{3,2,0,1:T(8,128)(2,1)} collective-permute-done((bf16[2,2,192,512]{3,2,0,1:T(8,128)(2,1)}, bf16[2,2,192,512]{3,2,0,1:T(8,128)(2,1)}, u32[]{:S(2)}, u32[]{:S(2)}) %collective-permute-start.13) | collective-permute-done | bytes 786464 | tf_op jit(solution)/shard_map/ppermute | solution.py:64
  173.7 1.3 constant_dynamic-update-slice_fusion.14
  175.0 1.3 constant_dynamic-update-slice_fusion.13
  176.3 1.2 constant_dynamic-update-slice_fusion.12
  185.0 4.0 constant_dynamic-slice_fusion.2
  189.0 4.4 %gather_fusion.2 = bf16[24,128,512]{2,1,0:T(8,128)(2,1)} fusion(bf16[24,128,512]{2,1,0:T(8,128)(2,1)} %bitcast.98, s32[1024]{0:T(1024)S(1)} %pad_clamp_fusion.3), kind=kCustom, calls=%fused_computation.2.clone | custom fusion | bytes 6291552 | tf_op jit(solution)/shard_map/jit(_take)/gather | solution.py:77
  193.5 2.3 select_select_fusion.1
  195.8 9.0 %fusion = bf16[1,1536,512]{1,2,0:T(8,128)(2,1)} fusion(bf16[3072,512]{1,0:T(8,128)(2,1)S(1)} %bitcast.101, bf16[1536,3072]{1,0:T(8,128)(2,1)} %param.20), kind=kOutput, calls=%fused_computation.32 | convolution fusion | flops 4832624640 | bytes 14155776 | tf_op jit(solution)/shard_map/dot_general | solution.py:79
  204.8 4.4 %gather_fusion.5 = bf16[24,128,512]{2,1,0:T(8,128)(2,1)} fusion(bf16[24,128,512]{2,1,0:T(8,128)(2,1)} %bitcast.97, s32[1024]{0:T(1024)S(1)} %pad_clamp_fusion.2), kind=kCustom, calls=%fused_computation.7.clone | custom fusion | bytes 6291552 | tf_op jit(solution)/shard_map/jit(_take)/gather | solution.py:77
  209.2 2.3 select_select_fusion
  211.5 8.0 %fusion.1 = bf16[1,1536,512]{1,2,0:T(8,128)(2,1)S(1)} fusion(bf16[3072,512]{1,0:T(8,128)(2,1)S(1)} %bitcast.102, bf16[1536,3072]{1,0:T(8,128)(2,1)} %param.20), kind=kOutput, calls=%fused_computation.33 | convolution fusion | flops 4832624640 | bytes 14155776 | tf_op jit(solution)/shard_map/dot_general | solution.py:79
  219.5 1.9 pad_maximum_fusion
  223.6 46.6 %reduce-scatter.2.cloned.1.call-done = bf16[2,1536,128]{1,2,0:T(8,128)(2,1)} async-done(((bf16[2,1536,512]{1,2,0:T(8,128)(2,1)}), bf16[2,1536,128]{1,2,0:T(8,128)(2,1)}) %reduce-scatter.2.cloned.1.call-update) | async-done | bytes 786448 | tf_op jit(solution)/shard_map/reduce_scatter | solution.py:82
  270.1 1.3 convert_element_type.45
  277.6 2.5 fusion.37
  280.1 13.1 %all-gather.3.cloned.1.call-done = bf16[1536,512]{0,1:T(8,128)(2,1)} async-done(((bf16[1536,128]{0,1:T(8,128)(2,1)}), bf16[1536,512]{0,1:T(8,128)(2,1)}) %all-gather.3.cloned.1.call-update) | async-done | bytes 1572880 | tf_op jit(solution)/shard_map/all_gather | solution.py:94
  293.2 2.0 fusion.4
  295.5 1.4 gather_fusion.10
  300.9 2.6 copy.27
  303.5 2.1 gather_fusion.6
  305.6 1.4 select_select_fusion.3
  307.0 69.1 %all-reduce.3.cloned.1.call-done = (f32[128,512]{1,0:T(8,128)}, f32[128,512]{1,0:T(8,128)}, f32[128,512]{1,0:T(8,128)}) async-done(((f32[128,512]{1,0:T(8,128)}, f32[128,512]{1,0:T(8,128)}, f32[128,512]{1,0:T(8,128)}), (f32[128,512]{1,0:T(8,128)}, f32[128,512]{1,0:T(8,128)}, f32[128,512]{1,0:T(8,128)})) %all-reduce.3.cloned.1.call-update) | async-done | bytes 786448 | tf_op jit(solution)/shard_map/psum | solution.py:100
  377.1 1.4 fusion.6
  378.5 7.1 %all_gather.11 = bf16[512,512]{1,0:T(8,128)(2,1)S(1)} all-gather(bf16[128,512]{1,0:T(8,128)(2,1)S(1)} %fusion.6), channel_id=1, replica_groups=mesh['row'=8,'col'=4] {'col'}, dimensions={0}, use_global_device_ids=true | all-gather | bytes 655360 | tf_op jit(solution)/shard_map/all_gather | solution.py:115
  385.7 1.9 convolution_subtract_fusion
  387.6 8.7 %all-gather.5.cloned.1.call-done = bf16[1536,512]{0,1:T(8,128)(2,1)} async-done(((bf16[1536,128]{0,1:T(8,128)(2,1)}), bf16[1536,512]{0,1:T(8,128)(2,1)}) %all-gather.5.cloned.1.call-update) | async-done | bytes 1572880 | tf_op jit(solution)/shard_map/all_gather | solution.py:99
  396.3 2.6 copy.30
  398.9 2.1 gather_fusion.8
  401.0 1.4 select_select_fusion.2
  (127 shorter events, 36.8 us)
Async XLA Ops:
  7.2 286.1 %copy-start = (bf16[512,512]{1,0:T(8,128)(2,1)S(1)}, bf16[512,512]{1,0:T(8,128)(2,1)}, u32[]{:S(2)}) copy-start(bf16[512,512]{1,0:T(8,128)(2,1)} %param.27) | copy-start | bytes 1572868
  7.2 19.4 %copy-start.3 = (bf16[1536,512]{1,0:T(8,128)(2,1)S(1)}, bf16[1536,512]{1,0:T(8,128)(2,1)}, u32[]{:S(2)}) copy-start(bf16[1536,512]{1,0:T(8,128)(2,1)} %param.26) | copy-start | bytes 4718596
  7.2 263.0 %reduce-scatter.2.cloned.1.call-start = ((), (), s32[]{:S(2)}) async-start(), calls=%async_computation.1 | async-start | bytes 3932160 | tf_op jit(solution)/shard_map/reduce_scatter | solution.py:82
  10.2 19.1 %collective-permute-start = (bf16[2,192,512]{2,1,0:T(8,128)(2,1)}, bf16[2,192,512]{2,1,0:T(8,128)(2,1)}, u32[]{:S(2)}, u32[]{:S(2)}) collective-permute-start(bf16[2,192,512]{2,1,0:T(8,128)(2,1)} %get-tuple-element.26), channel_id=1, source_target_pairs={{0,4},{5,9},{10,14},{15,19},{16,20},{21,25},{26,30},{31,3}} | collective-permute-start | bytes 1179656 | tf_op jit(solution)/shard_map/ppermute | solution.py:50
  15.9 15.8 %collective-permute-start.1 = (bf16[2,192,512]{2,1,0:T(8,128)(2,1)}, bf16[2,192,512]{2,1,0:T(8,128)(2,1)}, u32[]{:S(2)}, u32[]{:S(2)}) collective-permute-start(bf16[2,192,512]{2,1,0:T(8,128)(2,1)} %get-tuple-element.27), channel_id=1, source_target_pairs={{0,8},{5,13},{10,18},{15,23},{16,24},{21,29},{26,2},{31,7}} | collective-permute-start | bytes 1179656 | tf_op jit(solution)/shard_map/ppermute | solution.py:50
  17.9 16.2 %collective-permute-start.2 = (bf16[2,192,512]{2,1,0:T(8,128)(2,1)}, bf16[2,192,512]{2,1,0:T(8,128)(2,1)}, u32[]{:S(2)}, u32[]{:S(2)}) collective-permute-start(bf16[2,192,512]{2,1,0:T(8,128)(2,1)} %get-tuple-element.28), channel_id=1, source_target_pairs={{0,12},{5,17},{10,22},{15,27},{16,28},{21,1},{26,6},{31,11}} | collective-permute-start | bytes 1179656 | tf_op jit(solution)/shard_map/ppermute | solution.py:50
  20.0 15.2 %collective-permute-start.3 = (bf16[2,192,512]{2,1,0:T(8,128)(2,1)S(1)}, bf16[2,192,512]{2,1,0:T(8,128)(2,1)}, u32[]{:S(2)}, u32[]{:S(2)}) collective-permute-start(bf16[2,192,512]{2,1,0:T(8,128)(2,1)S(1)} %get-tuple-element.29), channel_id=1, source_target_pairs={{0,16},{5,21},{10,26},{15,31},{16,0},{21,5},{26,10},{31,15}} | collective-permute-start | bytes 1179656 | tf_op jit(solution)/shard_map/ppermute | solution.py:50
  24.5 11.7 %collective-permute-start.4 = (bf16[2,192,512]{2,1,0:T(8,128)(2,1)S(1)}, bf16[2,192,512]{2,1,0:T(8,128)(2,1)}, u32[]{:S(2)}, u32[]{:S(2)}) collective-permute-start(bf16[2,192,512]{2,1,0:T(8,128)(2,1)S(1)} %get-tuple-element.30), channel_id=1, source_target_pairs={{0,20},{5,25},{10,30},{15,3},{16,4},{21,9},{26,14},{31,19}} | collective-permute-start | bytes 1179656 | tf_op jit(solution)/shard_map/ppermute | solution.py:50
  28.2 2.5 copy-start.13
  29.4 10.1 %collective-permute-start.5 = (bf16[2,192,512]{2,1,0:T(8,128)(2,1)S(1)}, bf16[2,192,512]{2,1,0:T(8,128)(2,1)S(1)}, u32[]{:S(2)}, u32[]{:S(2)}) collective-permute-start(bf16[2,192,512]{2,1,0:T(8,128)(2,1)S(1)} %fusion.16), channel_id=1, source_target_pairs={{0,24},{5,29},{10,2},{15,7},{16,8},{21,13},{26,18},{31,23}} | collective-permute-start | bytes 1179656 | tf_op jit(solution)/shard_map/ppermute | solution.py:50
  31.7 12.0 %collective-permute-start.6 = (bf16[2,192,512]{2,1,0:T(8,128)(2,1)S(1)}, bf16[2,192,512]{2,1,0:T(8,128)(2,1)S(1)}, u32[]{:S(2)}, u32[]{:S(2)}) collective-permute-start(bf16[2,192,512]{2,1,0:T(8,128)(2,1)S(1)} %get-tuple-element.25), channel_id=1, source_target_pairs={{0,28},{5,1},{10,6},{15,11},{16,12},{21,17},{26,22},{31,27}} | collective-permute-start | bytes 1179656 | tf_op jit(solution)/shard_map/ppermute | solution.py:50
  35.1 67.0 %copy-start.1 = (s32[8]{0:T(128)S(1)}, s32[8]{0:T(128)}, u32[]{:S(2)}) copy-start(s32[8]{0:T(128)} %param.22) | copy-start | bytes 100
  36.2 84.3 %copy-start.16 = (s32[8,12]{1,0:T(8,128)S(1)}, s32[8,12]{1,0:T(8,128)}, u32[]{:S(2)}) copy-start(s32[8,12]{1,0:T(8,128)} %param.21) | copy-start | bytes 1156
  36.2 84.8 %copy-start.17 = (s32[8,12]{1,0:T(8,128)S(1)}, s32[8,12]{1,0:T(8,128)}, u32[]{:S(2)}) copy-start(s32[8,12]{1,0:T(8,128)} %param.24) | copy-start | bytes 1156
  36.2 85.4 %copy-start.2 = (s32[8]{0:T(128)S(1)}, s32[8]{0:T(128)}, u32[]{:S(2)}) copy-start(s32[8]{0:T(128)} %param.25) | copy-start | bytes 100
  43.9 20.0 %collective-permute-start.7 = (bf16[2,2,192,512]{3,2,0,1:T(8,128)(2,1)S(1)}, bf16[2,2,192,512]{3,2,0,1:T(8,128)(2,1)S(1)}, u32[]{:S(2)}, u32[]{:S(2)}) collective-permute-start(bf16[2,2,192,512]{3,2,0,1:T(8,128)(2,1)S(1)} %pad_maximum_fusion.1), channel_id=1, source_target_pairs={{0,4},{4,8},{8,12},{12,16},{16,20},{20,24},{24,28},{28,0},{1,5},{5... | collective-permute-start | bytes 2359304 | tf_op jit(solution)/shard_map/ppermute | solution.py:64
  63.9 0.9 copy-start.6
  64.8 18.6 %collective-permute-start.8 = (bf16[2,2,192,512]{3,2,0,1:T(8,128)(2,1)S(1)}, bf16[2,2,192,512]{3,2,0,1:T(8,128)(2,1)S(1)}, u32[]{:S(2)}, u32[]{:S(2)}) collective-permute-start(bf16[2,2,192,512]{3,2,0,1:T(8,128)(2,1)S(1)} %collective-permute-done.7), channel_id=1, source_target_pairs={{0,4},{4,8},{8,12},{12,16},{16,20},{20,24},{24,28},{28,0},{1,5},{5... | collective-permute-start | bytes 2359304 | tf_op jit(solution)/shard_map/ppermute | solution.py:64
  83.4 0.9 copy-start.8
  84.3 17.9 %collective-permute-start.9 = (bf16[2,2,192,512]{3,2,0,1:T(8,128)(2,1)S(1)}, bf16[2,2,192,512]{3,2,0,1:T(8,128)(2,1)}, u32[]{:S(2)}, u32[]{:S(2)}) collective-permute-start(bf16[2,2,192,512]{3,2,0,1:T(8,128)(2,1)S(1)} %collective-permute-done.8), channel_id=1, source_target_pairs={{0,4},{4,8},{8,12},{12,16},{16,20},{20,24},{24,28},{28,0},{1,5},{5... | collective-permute-start | bytes 2359304 | tf_op jit(solution)/shard_map/ppermute | solution.py:64
  102.1 17.4 %collective-permute-start.10 = (bf16[2,2,192,512]{3,2,0,1:T(8,128)(2,1)}, bf16[2,2,192,512]{3,2,0,1:T(8,128)(2,1)}, u32[]{:S(2)}, u32[]{:S(2)}) collective-permute-start(bf16[2,2,192,512]{3,2,0,1:T(8,128)(2,1)} %collective-permute-done.9), channel_id=1, source_target_pairs={{0,4},{4,8},{8,12},{12,16},{16,20},{20,24},{24,28},{28,0},{1,5},{5... | collective-permute-start | bytes 2359304 | tf_op jit(solution)/shard_map/ppermute | solution.py:64
  119.6 16.6 %collective-permute-start.11 = (bf16[2,2,192,512]{3,2,0,1:T(8,128)(2,1)}, bf16[2,2,192,512]{3,2,0,1:T(8,128)(2,1)}, u32[]{:S(2)}, u32[]{:S(2)}) collective-permute-start(bf16[2,2,192,512]{3,2,0,1:T(8,128)(2,1)} %collective-permute-done.10), channel_id=1, source_target_pairs={{0,4},{4,8},{8,12},{12,16},{16,20},{20,24},{24,28},{28,0},{1,5},{5... | collective-permute-start | bytes 2359304 | tf_op jit(solution)/shard_map/ppermute | solution.py:64
  136.2 18.6 %collective-permute-start.12 = (bf16[2,2,192,512]{3,2,0,1:T(8,128)(2,1)}, bf16[2,2,192,512]{3,2,0,1:T(8,128)(2,1)}, u32[]{:S(2)}, u32[]{:S(2)}) collective-permute-start(bf16[2,2,192,512]{3,2,0,1:T(8,128)(2,1)} %collective-permute-done.11), channel_id=1, source_target_pairs={{0,4},{4,8},{8,12},{12,16},{16,20},{20,24},{24,28},{28,0},{1,5},{5... | collective-permute-start | bytes 2359304 | tf_op jit(solution)/shard_map/ppermute | solution.py:64
  154.8 17.7 %collective-permute-start.13 = (bf16[2,2,192,512]{3,2,0,1:T(8,128)(2,1)}, bf16[2,2,192,512]{3,2,0,1:T(8,128)(2,1)}, u32[]{:S(2)}, u32[]{:S(2)}) collective-permute-start(bf16[2,2,192,512]{3,2,0,1:T(8,128)(2,1)} %collective-permute-done.12), channel_id=1, source_target_pairs={{0,4},{4,8},{8,12},{12,16},{16,20},{20,24},{24,28},{28,0},{1,5},{5... | collective-permute-start | bytes 2359304 | tf_op jit(solution)/shard_map/ppermute | solution.py:64
  173.7 4.9 %copy-start.9 = (bf16[2,2,192,512]{3,2,0,1:T(8,128)(2,1)S(1)}, bf16[2,2,192,512]{3,2,0,1:T(8,128)(2,1)}, u32[]{:S(2)}) copy-start(bf16[2,2,192,512]{3,2,0,1:T(8,128)(2,1)} %copy-done.8) | copy-start | bytes 2359300
  175.0 3.7 copy-start.7
  211.5 8.0 %copy-start.10 = (bf16[1,1536,512]{1,2,0:T(8,128)(2,1)S(1)}, bf16[1,1536,512]{1,2,0:T(8,128)(2,1)}, u32[]{:S(2)}) copy-start(bf16[1,1536,512]{1,2,0:T(8,128)(2,1)} %fusion) | copy-start | bytes 4718596
  221.5 71.8 %all-gather.3.cloned.1.call-start = ((), (), s32[]{:S(2)}) async-start(), calls=%async_computation.2 | async-start | bytes 1966080 | tf_op jit(solution)/shard_map/all_gather | solution.py:94
  271.5 1.1 copy-start.4
  273.4 102.7 %all-reduce.3.cloned.1.call-start = ((), (), s32[]{:S(2)}) async-start(), calls=%async_computation.4 | async-start | bytes 1572864 | tf_op jit(solution)/shard_map/psum | solution.py:100
  295.3 5.0 %copy-start.5 = (bf16[1536,128]{0,1:T(8,128)(2,1)}, bf16[1536,128]{0,1:T(8,128)(2,1)S(1)}, u32[]{:S(2)}) copy-start(bf16[1536,128]{0,1:T(8,128)(2,1)S(1)} %fusion.4) | copy-start | bytes 1179652
  300.3 96.0 %all-gather.5.cloned.1.call-start = ((), (), s32[]{:S(2)}) async-start(), calls=%async_computation.3 | async-start | bytes 1966080 | tf_op jit(solution)/shard_map/all_gather | solution.py:99
  303.5 72.6 %copy-start.14 = (f32[128,512]{1,0:T(8,128)S(1)}, f32[128,512]{1,0:T(8,128)}, u32[]{:S(2)}) copy-start(f32[128,512]{1,0:T(8,128)} %param.28) | copy-start | bytes 786436
  305.6 80.1 %copy-start.15 = (f32[128,512]{1,0:T(8,128)S(1)}, f32[128,512]{1,0:T(8,128)}, u32[]{:S(2)}) copy-start(f32[128,512]{1,0:T(8,128)} %param.29) | copy-start | bytes 786436
  377.1 21.8 %copy-start.11 = (f32[128,512]{1,0:T(8,128)}, f32[128,512]{1,0:T(8,128)S(1)}, u32[]{:S(2)}) copy-start(f32[128,512]{1,0:T(8,128)S(1)} %sub.23) | copy-start | bytes 786436
  378.5 22.5 %copy-start.12 = (bf16[128,512]{1,0:T(8,128)(2,1)}, bf16[128,512]{1,0:T(8,128)(2,1)S(1)}, u32[]{:S(2)}) copy-start(bf16[128,512]{1,0:T(8,128)(2,1)S(1)} %fusion.6) | copy-start | bytes 393220
Sparse Core Ops, SparseCore 0:
  221.6 48.5 reduce-scatter.1
  273.6 19.6 all-gather.2
  300.4 75.6 all-reduce.2
  377.5 18.7 all-gather.4
